TPU v7x, 256 devices: a whole 4x4x8 slice. The times are simulated.
256 devices in a mesh: dp: 32 (over x_hi, z, core), tensor: 8 (over y, x_lo).
Axes of the slice: x: 4 (x_hi: 2, x_lo: 2; x = x_hi * 2 + x_lo), y: 4, z: 8, core: 2. Of those that a mesh axis runs over, the one named last changes fastest.
Arguments:
- tokens: bfloat16 [32768, 8192], P(('dp', 'tensor')), may hold values from -6 to 6
- out_grad: bfloat16 [32768, 26624], P('dp', 'tensor')
- delta: float32 [8, 128, 128, 128], P('tensor', 'dp'), may hold values from -3 to 3
- block_rows: int32 [1024], P('tensor'), may hold values from 0 to 63, as said below
- block_cols: int32 [1024], P('tensor'), may hold values from 0 to 25, as said below
- block_count: int32 [8], P('tensor'), may hold values from 1 to 128, as said below
Outputs:
- new_delta: float32 [8, 128, 128, 128], P('tensor', 'dp')
Inputs may be any that keep to these rules, and one draw needn't show every extreme that they name: `block_rows`: entry t * 128 + k names the row block of slot k of tensor shard t; the slots of one shard name distinct pairs of row and column block. `block_cols`: entry t * 128 + k names the column block, counted within shard t's columns, of slot k of shard t. Slots 0 to block_count[t] - 1 of shard t are live, the rest are padding; some shard has all 128 live.
All inputs are finite; a program needn't handle non-finite values.
Results may differ from a plain program's by a relative error of at most 0.0003.
Values may be sent and summed in bfloat16 or wider, within the bound.
No kernel may reach another device: no remote copies, remote signals or barrier semaphores. Data moves between devices by JAX's collectives and lax.ppermute only.
A program may use at most 192 MiB of HBM per device.

v0:
```python
import math
import jax
import jax.numpy as jnp
from jax import lax
from jax.sharding import PartitionSpec as P

GROUP = 32


def on_device(tokens, out_grad, delta, block_rows, block_cols, block_count):
    slot_count = block_rows.shape[0]
    block_size = delta.shape[-1]
    row_blocks = tokens.shape[1] // block_size
    col_blocks = out_grad.shape[1] // block_size
    group_trips = slot_count // GROUP
    zero_grads = jnp.zeros((slot_count, block_size, block_size), jnp.float32)
    shard_rows = lax.all_gather(tokens, "tensor", axis=0, tiled=True)
    row_count = shard_rows.shape[0]
    token_tiles = shard_rows.reshape(row_count, row_blocks, block_size)
    grad_tiles = out_grad.reshape(row_count, col_blocks, block_size)

    def one_group(group_index, partial_sum):
        row_ids = lax.dynamic_slice_in_dim(block_rows, group_index * GROUP, GROUP)
        col_ids = lax.dynamic_slice_in_dim(block_cols, group_index * GROUP, GROUP)
        token_cols = jnp.take(token_tiles, row_ids, axis=1)
        grad_cols = jnp.take(grad_tiles, col_ids, axis=1)
        partial_value = jnp.einsum(
            "rkc,rkd->kcd", token_cols, grad_cols, preferred_element_type=jnp.float32
        )
        previous = lax.dynamic_slice_in_dim(partial_sum, group_index * GROUP, GROUP, 0)
        return lax.dynamic_update_slice_in_dim(
            partial_sum, previous + partial_value, group_index * GROUP, 0
        )

    block_grads = lax.fori_loop(0, group_trips, one_group, zero_grads)
    live_mask = (jnp.arange(slot_count, dtype=jnp.int32) < block_count[0]).astype(jnp.float32)
    block_grads = block_grads * live_mask[:, None, None]
    cycle_size = lax.axis_size("tensor")
    norm_limit = block_size * math.sqrt(cycle_size * slot_count)
    share_len = delta.shape[1]
    summed = lax.psum(block_grads, "dp")
    square_sum = lax.psum(jnp.sum(summed * summed), "tensor")
    own_share = lax.dynamic_slice_in_dim(summed, lax.axis_index("dp") * share_len, share_len, 0)
    factor = jnp.minimum(jnp.float32(1.0), norm_limit / jnp.sqrt(square_sum + 1e-06))
    return delta - 0.5 * factor * own_share[None]


def solution(mesh):
    return jax.shard_map(
        on_device,
        mesh=mesh,
        in_specs=(
            P(("dp", "tensor"), None),
            P("dp", "tensor"),
            P("tensor", "dp", None, None),
            P("tensor"),
            P("tensor"),
            P("tensor"),
        ),
        out_specs=P("tensor", "dp", None, None),
        check_vma=False,
    )
```

profile of v0, /device:TPU:4, one launch (start us, length us, event | category | flops | bytes accessed | tf_op | source)
XLA Modules:
  0.0 820.9 jit_solution(13977758874296105967)
XLA Ops:
  6.5 4.1 copy.13
  10.7 10.0 %copy.14 = bf16[1024,3328]{0,1:T(8,128)(2,1)} copy(bf16[1024,3328]{1,0:T(8,128)(2,1)} %param.9) | data formatting | bytes 13631488 | tf_op args[1]
  20.7 10.0 %copy.16 = bf16[1024,26,128]{2,0,1:T(8,128)(2,1)} copy(bf16[1024,26,128]{0,2,1:T(8,128)(2,1)} %bitcast.20) | data formatting | bytes 13631488 | tf_op jit(solution)/shard_map/while | solution.py:35
  31.3 310.0 %all-gather.2.cloned.1.call-done = bf16[1024,8192]{0,1:T(8,128)(2,1)} async-done(((bf16[128,8192]{0,1:T(8,128)(2,1)}), bf16[1024,8192]{0,1:T(8,128)(2,1)}) %all-gather.2.cloned.1.call-update) | async-done | bytes 16777232 | tf_op jit(solution)/shard_map/all_gather | solution.py:17
  341.3 22.4 %copy.15 = bf16[1024,64,128]{2,0,1:T(8,128)(2,1)} copy(bf16[1024,64,128]{0,2,1:T(8,128)(2,1)} %bitcast.21) | data formatting | bytes 33554432 | tf_op jit(solution)/shard_map/while | solution.py:35
  363.7 4.3 broadcast_in_dim.47
  368.0 118.7 %while.13 = (s32[]{:T(128)}, f32[128,128,128]{2,1,0:T(8,128)}, s32[128]{0:T(128)S(1)}, bf16[1024,64,128]{2,0,1:T(8,128)(2,1)}, s32[128]{0:T(128)S(1)}, /*index=5...) while((s32[]{:T(128)}, f32[128,128,128]{2,1,0:T(8,128)}, s32[128]{0:T(128)S(1)}, ...), condition=%wide.region_1.0_spmd, body=%wide.region_0.1_spmd.sunk | while | flops 1082657152 | bytes 54535460 | solution.py:35
  368.0 8.0 gather_fusion
  376.0 10.8 %gather_fusion.1 = bf16[32,1024,128]{2,1,0:T(8,128)(2,1)} fusion(bf16[1024,64,128]{2,0,1:T(8,128)(2,1)} %get-tuple-element.213, s32[1024]{0:T(1024)S(1)} %pad_clamp_fusion.5), kind=kCustom, calls=%fused_computation.clone.1 | custom fusion | bytes 16777344 | tf_op jit(solution)/shard_map/while/body/eval_jaxpr/jit(_take)/gather | solution.py:25
  386.8 10.8 %add_dynamic-update-slice_fusion.2 = f32[128,128,128]{2,1,0:T(8,128)} fusion(f32[128,128,128]{2,1,0:T(8,128)} %get-tuple-element.201, s32[]{:T(128)S(6)} %select_n.70, bf16[32,1024,128]{2,1,0:T(8,128)(2,1)} %gather_fusion, pred[32]{0:T(512)(128)(4,1)S(1)} %get-tuple-element.187, bf16[32,1024,128]{2,1,0:T(8,128)(2,1)} %gather_fusion.1, ...), kind=kOutput, calls=%fused_computation.10.clone.1 | convolution fusion | flops 1082654720 | bytes 20971588 | tf_op jit(solution)/shard_map/while/body/eval_jaxpr/rkc,rkd->kcd/dot_general | solution.py:27
  397.7 8.0 gather_fusion
  405.7 10.8 %gather_fusion.1 = bf16[32,1024,128]{2,1,0:T(8,128)(2,1)} fusion(bf16[1024,64,128]{2,0,1:T(8,128)(2,1)} %get-tuple-element.213, s32[1024]{0:T(1024)S(1)} %pad_clamp_fusion.5), kind=kCustom, calls=%fused_computation.clone.1 | custom fusion | bytes 16777344 | tf_op jit(solution)/shard_map/while/body/eval_jaxpr/jit(_take)/gather | solution.py:25
  416.4 10.9 %add_dynamic-update-slice_fusion.2 = f32[128,128,128]{2,1,0:T(8,128)} fusion(f32[128,128,128]{2,1,0:T(8,128)} %get-tuple-element.201, s32[]{:T(128)S(6)} %select_n.70, bf16[32,1024,128]{2,1,0:T(8,128)(2,1)} %gather_fusion, pred[32]{0:T(512)(128)(4,1)S(1)} %get-tuple-element.187, bf16[32,1024,128]{2,1,0:T(8,128)(2,1)} %gather_fusion.1, ...), kind=kOutput, calls=%fused_computation.10.clone.1 | convolution fusion | flops 1082654720 | bytes 20971588 | tf_op jit(solution)/shard_map/while/body/eval_jaxpr/rkc,rkd->kcd/dot_general | solution.py:27
  427.4 7.9 gather_fusion
  435.3 10.8 %gather_fusion.1 = bf16[32,1024,128]{2,1,0:T(8,128)(2,1)} fusion(bf16[1024,64,128]{2,0,1:T(8,128)(2,1)} %get-tuple-element.213, s32[1024]{0:T(1024)S(1)} %pad_clamp_fusion.5), kind=kCustom, calls=%fused_computation.clone.1 | custom fusion | bytes 16777344 | tf_op jit(solution)/shard_map/while/body/eval_jaxpr/jit(_take)/gather | solution.py:25
  446.1 10.8 %add_dynamic-update-slice_fusion.2 = f32[128,128,128]{2,1,0:T(8,128)} fusion(f32[128,128,128]{2,1,0:T(8,128)} %get-tuple-element.201, s32[]{:T(128)S(6)} %select_n.70, bf16[32,1024,128]{2,1,0:T(8,128)(2,1)} %gather_fusion, pred[32]{0:T(512)(128)(4,1)S(1)} %get-tuple-element.187, bf16[32,1024,128]{2,1,0:T(8,128)(2,1)} %gather_fusion.1, ...), kind=kOutput, calls=%fused_computation.10.clone.1 | convolution fusion | flops 1082654720 | bytes 20971588 | tf_op jit(solution)/shard_map/while/body/eval_jaxpr/rkc,rkd->kcd/dot_general | solution.py:27
  457.0 7.9 gather_fusion
  465.0 10.8 %gather_fusion.1 = bf16[32,1024,128]{2,1,0:T(8,128)(2,1)} fusion(bf16[1024,64,128]{2,0,1:T(8,128)(2,1)} %get-tuple-element.213, s32[1024]{0:T(1024)S(1)} %pad_clamp_fusion.5), kind=kCustom, calls=%fused_computation.clone.1 | custom fusion | bytes 16777344 | tf_op jit(solution)/shard_map/while/body/eval_jaxpr/jit(_take)/gather | solution.py:25
  475.8 10.8 %add_dynamic-update-slice_fusion.2 = f32[128,128,128]{2,1,0:T(8,128)} fusion(f32[128,128,128]{2,1,0:T(8,128)} %get-tuple-element.201, s32[]{:T(128)S(6)} %select_n.70, bf16[32,1024,128]{2,1,0:T(8,128)(2,1)} %gather_fusion, pred[32]{0:T(512)(128)(4,1)S(1)} %get-tuple-element.187, bf16[32,1024,128]{2,1,0:T(8,128)(2,1)} %gather_fusion.1, ...), kind=kOutput, calls=%fused_computation.10.clone.1 | convolution fusion | flops 1082654720 | bytes 20971588 | tf_op jit(solution)/shard_map/while/body/eval_jaxpr/rkc,rkd->kcd/dot_general | solution.py:27
  486.6 7.2 broadcast_multiply_fusion
  493.9 291.6 %all-reduce.2.cloned.1.call-done = f32[128,128,128]{2,1,0:T(8,128)} async-done(((f32[128,128,128]{2,1,0:T(8,128)}), f32[128,128,128]{2,1,0:T(8,128)}) %all-reduce.2.cloned.1.call-update) | async-done | bytes 8388624 | tf_op jit(solution)/shard_map/psum | solution.py:41
  785.5 6.1 multiply_reduce_fusion
  791.6 20.0 %psum.15 = f32[]{:T(128)} all-reduce(f32[]{:T(128)} %multiply_reduce_fusion), channel_id=1, replica_groups=mesh['dp'=32,'tensor'=8] {'tensor'}, use_global_device_ids=true, to_apply=%region_4.5 | all-reduce | flops 1 | bytes 8 | tf_op jit(solution)/shard_map/psum | solution.py:42
  812.3 1.7 bitcast_subtract_fusion
  (23 shorter events, 0.5 us)
Async XLA Ops:
  6.5 334.8 %all-gather.2.cloned.1.call-start = ((), (), s32[]{:S(2)}) async-start(), calls=%async_computation | async-start | bytes 18874368 | tf_op jit(solution)/shard_map/all_gather | solution.py:17
  10.6 774.8 %all-reduce.2.cloned.1.call-start = ((), (), s32[]{:S(2)}) async-start(), calls=%async_computation.1 | async-start | bytes 16777216 | tf_op jit(solution)/shard_map/psum | solution.py:41
  363.7 4.3 copy-start.1
  363.7 4.3 copy-start.2
  493.8 318.5 %copy-start = (f32[1,4,128,128]{3,2,1,0:T(8,128)S(1)}, f32[1,4,128,128]{3,2,1,0:T(8,128)}, u32[]{:S(2)}) copy-start(f32[1,4,128,128]{3,2,1,0:T(8,128)} %param.10) | copy-start | bytes 786436
Sparse Core Ops, SparseCore 0:
  10.8 330.4 all-gather.1
  494.0 291.4 all-reduce.1
where the time goes:
time: 822 us; the launch traced here: 821 us
  waiting for transfers between devices  602 us (73%)
  local copies, waits for them, and re-layouts  126 us (15%)
  matrix products  43.4 us (5%)
  blocking collectives  20 us (2%)
  other arithmetic  15.4 us (2%)
  between operations  14.8 us (2%)
    all_gather x1, waiting for transfers between devices, on_device(): shard_rows = lax.all_gather(tokens, 'tensor', axis=0, tiled=True)  310 us
    psum x1, waiting for transfers between devices, on_device(): summed = lax.psum(block_grads, 'dp')  292 us
    dot_general x4, matrix products, one_group(): jnp.einsum('rkc,rkd->kcd', token_cols, grad_cols, preferred_element_type=...  43.4 us
    gather x4, local copies, waits for them, and re-layouts, one_group(): token_cols = jnp.take(token_tiles, row_ids, axis=1)  43.1 us
    while x2, local copies, waits for them, and re-layouts, on_device(): block_grads = lax.fori_loop(0, group_trips, one_group, zero_grads)  32.4 us
    gather x4, local copies, waits for them, and re-layouts, one_group(): grad_cols = jnp.take(grad_tiles, col_ids, axis=1)  31.8 us
    psum x1, blocking collectives, on_device(): square_sum = lax.psum(jnp.sum(summed * summed), 'tensor')  20 us
  transfers between devices with their start and end apart: 2, of which 2 were waited for; matrix products, arithmetic and copies ran while one was open for 2% of the time, Pallas kernels for 0%

commit v1 on v0

--- a/solution.py
+++ b/solution.py
@@ -7,6 +7,11 @@
 GROUP = 32
 
 
+def swapped_in(block, name, along):
+    sent = jnp.stack([block] * lax.axis_size(name))
+    return jnp.concatenate(lax.all_to_all(sent, name, 0, 0), axis=along)
+
+
 def on_device(tokens, out_grad, delta, block_rows, block_cols, block_count):
     slot_count = block_rows.shape[0]
     block_size = delta.shape[-1]
@@ -14,7 +19,7 @@
     col_blocks = out_grad.shape[1] // block_size
     group_trips = slot_count // GROUP
     zero_grads = jnp.zeros((slot_count, block_size, block_size), jnp.float32)
-    shard_rows = lax.all_gather(tokens, "tensor", axis=0, tiled=True)
+    shard_rows = swapped_in(tokens, "tensor", 0)
     row_count = shard_rows.shape[0]
     token_tiles = shard_rows.reshape(row_count, row_blocks, block_size)
     grad_tiles = out_grad.reshape(row_count, col_blocks, block_size)

time: 822 us -> 708 us (0.86)
  waiting for transfers between devices: 602 us -> 456 us
  local copies, waits for them, and re-layouts: 126 us -> 151 us
    all_gather x1 -> x0, waiting for transfers between devices: 310 us -> none  [on_device(): shard_rows = lax.all_gather(tokens, 'tensor', axis=0, tiled=True)]
    all_to_all x0 -> x1, waiting for transfers between devices: none -> 164 us  [swapped_in(): return jnp.concatenate(lax.all_to_all(sent, name, 0, 0), axis=along)]
    while x2, local copies, waits for them, and re-layouts: 32.4 us -> 46 us  [on_device(): block_grads = lax.fori_loop(0, group_trips, one_group, zero_grads)]
  transfers between devices with their start and end apart: 2 -> 2, of which waited for: 2 -> 2; matrix products, arithmetic and copies ran while one was open for 2% -> 3% of each run, Pallas kernels for 0% -> 0%
where the time goes in v1:
time: 708 us; the launch traced here: 707 us
  waiting for transfers between devices  456 us (64%)
  local copies, waits for them, and re-layouts  151 us (21%)
  matrix products  43.4 us (6%)
  blocking collectives  20 us (3%)
  other arithmetic  15.4 us (2%)
  between operations  14.8 us (2%)
    psum x1, waiting for transfers between devices, on_device(): summed = lax.psum(block_grads, 'dp')  292 us
    all_to_all x1, waiting for transfers between devices, swapped_in(): return jnp.concatenate(lax.all_to_all(sent, name, 0, 0), axis=along)  164 us
    while x2, local copies, waits for them, and re-layouts, on_device(): block_grads = lax.fori_loop(0, group_trips, one_group, zero_grads)  46 us
    dot_general x4, matrix products, one_group(): jnp.einsum('rkc,rkd->kcd', token_cols, grad_cols, preferred_element_type=...  43.4 us
    gather x4, local copies, waits for them, and re-layouts, one_group(): token_cols = jnp.take(token_tiles, row_ids, axis=1)  43.1 us
    gather x4, local copies, waits for them, and re-layouts, one_group(): grad_cols = jnp.take(grad_tiles, col_ids, axis=1)  31.7 us
    psum x1, blocking collectives, on_device(): square_sum = lax.psum(jnp.sum(summed * summed), 'tensor')  20 us
    unnamed x8, local copies, waits for them, and re-layouts  19.7 us
  transfers between devices with their start and end apart: 2, of which 2 were waited for; matrix products, arithmetic and copies ran while one was open for 3% of the time, Pallas kernels for 0%

profile of v1, /device:TPU:4, one launch (start us, length us, event | category | flops | bytes accessed | tf_op | source)
XLA Modules:
  0.0 706.5 jit_solution(3680753333981385865)
XLA Ops:
  6.5 6.8 stack.2
  13.4 5.7 all-to-all-start
  19.2 10.0 %copy.13 = bf16[1024,3328]{0,1:T(8,128)(2,1)} copy(bf16[1024,3328]{1,0:T(8,128)(2,1)} %param.9) | data formatting | bytes 13631488 | tf_op args[1]
  29.1 9.9 %copy.15 = bf16[1024,26,128]{2,0,1:T(8,128)(2,1)} copy(bf16[1024,26,128]{0,2,1:T(8,128)(2,1)} %bitcast.23) | data formatting | bytes 13631488 | tf_op jit(solution)/shard_map/while | solution.py:40
  39.7 163.9 %all-to-all-done = bf16[8,128,8192]{2,1,0:T(8,128)(2,1)} async-done(((bf16[8,128,8192]{2,1,0:T(8,128)(2,1)}), bf16[8,128,8192]{2,1,0:T(8,128)(2,1)}, u32[]{:S(2)}, u32[]{:S(2)}) %all-to-all-start) | async-done | bytes 16777248 | tf_op jit(solution)/shard_map/all_to_all | solution.py:12
  203.7 9.7 %copy.17 = bf16[128,8,64,128]{3,2,1,0:T(8,128)(2,1)S(1)} copy(bf16[128,8,64,128]{3,1,2,0:T(8,128)(2,1)} %bitcast.6) | data formatting | bytes 33554432
  213.4 36.0 %copy.14 = bf16[1024,64,128]{2,0,1:T(8,128)(2,1)} copy(bf16[1024,64,128]{2,1,0:T(8,128)(2,1)S(1)} %bitcast.22) | data formatting | bytes 33554432 | tf_op jit(solution)/shard_map/while | solution.py:40
  253.7 118.6 %while.13 = (s32[]{:T(128)}, f32[128,128,128]{2,1,0:T(8,128)}, s32[128]{0:T(128)S(1)}, bf16[1024,64,128]{2,0,1:T(8,128)(2,1)}, s32[128]{0:T(128)S(1)}, /*index=5...) while((s32[]{:T(128)}, f32[128,128,128]{2,1,0:T(8,128)}, s32[128]{0:T(128)S(1)}, ...), condition=%wide.region_1.0_spmd, body=%wide.region_0.1_spmd.sunk | while | flops 1082657152 | bytes 54535460 | solution.py:40
  253.7 7.9 %gather_fusion = bf16[32,1024,128]{2,1,0:T(8,128)(2,1)} fusion(bf16[1024,26,128]{2,0,1:T(8,128)(2,1)} %get-tuple-element.215, s32[1024]{0:T(1024)S(1)} %pad_clamp_fusion.4), kind=kCustom, calls=%fused_computation.1.clone.1 | custom fusion | bytes 16777344 | tf_op jit(solution)/shard_map/while/body/eval_jaxpr/jit(_take)/gather | solution.py:31
  261.7 10.8 %gather_fusion.1 = bf16[32,1024,128]{2,1,0:T(8,128)(2,1)} fusion(bf16[1024,64,128]{2,0,1:T(8,128)(2,1)} %get-tuple-element.213, s32[1024]{0:T(1024)S(1)} %pad_clamp_fusion.5), kind=kCustom, calls=%fused_computation.clone.1 | custom fusion | bytes 16777344 | tf_op jit(solution)/shard_map/while/body/eval_jaxpr/jit(_take)/gather | solution.py:30
  272.5 10.8 %add_dynamic-update-slice_fusion.2 = f32[128,128,128]{2,1,0:T(8,128)} fusion(f32[128,128,128]{2,1,0:T(8,128)} %get-tuple-element.201, s32[]{:T(128)S(6)} %select_n.70, bf16[32,1024,128]{2,1,0:T(8,128)(2,1)} %gather_fusion, pred[32]{0:T(512)(128)(4,1)S(1)} %get-tuple-element.187, bf16[32,1024,128]{2,1,0:T(8,128)(2,1)} %gather_fusion.1, ...), kind=kOutput, calls=%fused_computation.10.clone.1 | convolution fusion | flops 1082654720 | bytes 20971588 | tf_op jit(solution)/shard_map/while/body/eval_jaxpr/rkc,rkd->kcd/dot_general | solution.py:32
  283.4 7.9 %gather_fusion = bf16[32,1024,128]{2,1,0:T(8,128)(2,1)} fusion(bf16[1024,26,128]{2,0,1:T(8,128)(2,1)} %get-tuple-element.215, s32[1024]{0:T(1024)S(1)} %pad_clamp_fusion.4), kind=kCustom, calls=%fused_computation.1.clone.1 | custom fusion | bytes 16777344 | tf_op jit(solution)/shard_map/while/body/eval_jaxpr/jit(_take)/gather | solution.py:31
  291.3 10.8 %gather_fusion.1 = bf16[32,1024,128]{2,1,0:T(8,128)(2,1)} fusion(bf16[1024,64,128]{2,0,1:T(8,128)(2,1)} %get-tuple-element.213, s32[1024]{0:T(1024)S(1)} %pad_clamp_fusion.5), kind=kCustom, calls=%fused_computation.clone.1 | custom fusion | bytes 16777344 | tf_op jit(solution)/shard_map/while/body/eval_jaxpr/jit(_take)/gather | solution.py:30
  302.1 10.9 %add_dynamic-update-slice_fusion.2 = f32[128,128,128]{2,1,0:T(8,128)} fusion(f32[128,128,128]{2,1,0:T(8,128)} %get-tuple-element.201, s32[]{:T(128)S(6)} %select_n.70, bf16[32,1024,128]{2,1,0:T(8,128)(2,1)} %gather_fusion, pred[32]{0:T(512)(128)(4,1)S(1)} %get-tuple-element.187, bf16[32,1024,128]{2,1,0:T(8,128)(2,1)} %gather_fusion.1, ...), kind=kOutput, calls=%fused_computation.10.clone.1 | convolution fusion | flops 1082654720 | bytes 20971588 | tf_op jit(solution)/shard_map/while/body/eval_jaxpr/rkc,rkd->kcd/dot_general | solution.py:32
  313.1 7.9 %gather_fusion = bf16[32,1024,128]{2,1,0:T(8,128)(2,1)} fusion(bf16[1024,26,128]{2,0,1:T(8,128)(2,1)} %get-tuple-element.215, s32[1024]{0:T(1024)S(1)} %pad_clamp_fusion.4), kind=kCustom, calls=%fused_computation.1.clone.1 | custom fusion | bytes 16777344 | tf_op jit(solution)/shard_map/while/body/eval_jaxpr/jit(_take)/gather | solution.py:31
  321.0 10.8 %gather_fusion.1 = bf16[32,1024,128]{2,1,0:T(8,128)(2,1)} fusion(bf16[1024,64,128]{2,0,1:T(8,128)(2,1)} %get-tuple-element.213, s32[1024]{0:T(1024)S(1)} %pad_clamp_fusion.5), kind=kCustom, calls=%fused_computation.clone.1 | custom fusion | bytes 16777344 | tf_op jit(solution)/shard_map/while/body/eval_jaxpr/jit(_take)/gather | solution.py:30
  331.8 10.8 %add_dynamic-update-slice_fusion.2 = f32[128,128,128]{2,1,0:T(8,128)} fusion(f32[128,128,128]{2,1,0:T(8,128)} %get-tuple-element.201, s32[]{:T(128)S(6)} %select_n.70, bf16[32,1024,128]{2,1,0:T(8,128)(2,1)} %gather_fusion, pred[32]{0:T(512)(128)(4,1)S(1)} %get-tuple-element.187, bf16[32,1024,128]{2,1,0:T(8,128)(2,1)} %gather_fusion.1, ...), kind=kOutput, calls=%fused_computation.10.clone.1 | convolution fusion | flops 1082654720 | bytes 20971588 | tf_op jit(solution)/shard_map/while/body/eval_jaxpr/rkc,rkd->kcd/dot_general | solution.py:32
  342.7 7.9 %gather_fusion = bf16[32,1024,128]{2,1,0:T(8,128)(2,1)} fusion(bf16[1024,26,128]{2,0,1:T(8,128)(2,1)} %get-tuple-element.215, s32[1024]{0:T(1024)S(1)} %pad_clamp_fusion.4), kind=kCustom, calls=%fused_computation.1.clone.1 | custom fusion | bytes 16777344 | tf_op jit(solution)/shard_map/while/body/eval_jaxpr/jit(_take)/gather | solution.py:31
  350.6 10.8 %gather_fusion.1 = bf16[32,1024,128]{2,1,0:T(8,128)(2,1)} fusion(bf16[1024,64,128]{2,0,1:T(8,128)(2,1)} %get-tuple-element.213, s32[1024]{0:T(1024)S(1)} %pad_clamp_fusion.5), kind=kCustom, calls=%fused_computation.clone.1 | custom fusion | bytes 16777344 | tf_op jit(solution)/shard_map/while/body/eval_jaxpr/jit(_take)/gather | solution.py:30
  361.4 10.8 %add_dynamic-update-slice_fusion.2 = f32[128,128,128]{2,1,0:T(8,128)} fusion(f32[128,128,128]{2,1,0:T(8,128)} %get-tuple-element.201, s32[]{:T(128)S(6)} %select_n.70, bf16[32,1024,128]{2,1,0:T(8,128)(2,1)} %gather_fusion, pred[32]{0:T(512)(128)(4,1)S(1)} %get-tuple-element.187, bf16[32,1024,128]{2,1,0:T(8,128)(2,1)} %gather_fusion.1, ...), kind=kOutput, calls=%fused_computation.10.clone.1 | convolution fusion | flops 1082654720 | bytes 20971588 | tf_op jit(solution)/shard_map/while/body/eval_jaxpr/rkc,rkd->kcd/dot_general | solution.py:32
  372.2 7.2 %broadcast_multiply_fusion = f32[128,128,128]{2,1,0:T(8,128)} fusion(f32[128,128,128]{2,1,0:T(8,128)} %get-tuple-element.114, f32[128]{0:T(128)S(1)} %compare_convert_fusion), kind=kLoop, calls=%fused_computation.19 | loop fusion | flops 2097152 | bytes 16777728 | tf_op jit(solution)/shard_map/mul | solution.py:42
  379.4 291.7 %all-reduce.2.cloned.1.call-done = f32[128,128,128]{2,1,0:T(8,128)} async-done(((f32[128,128,128]{2,1,0:T(8,128)}), f32[128,128,128]{2,1,0:T(8,128)}) %all-reduce.2.cloned.1.call-update) | async-done | bytes 8388624 | tf_op jit(solution)/shard_map/psum | solution.py:46
  671.1 6.1 multiply_reduce_fusion
  677.3 20.0 %psum.15 = f32[]{:T(128)} all-reduce(f32[]{:T(128)} %multiply_reduce_fusion), channel_id=1, replica_groups=mesh['dp'=32,'tensor'=8] {'tensor'}, use_global_device_ids=true, to_apply=%region_4.5 | all-reduce | flops 1 | bytes 8 | tf_op jit(solution)/shard_map/psum | solution.py:47
  (23 shorter events, 6.4 us)
Async XLA Ops:
  13.4 190.3 %all-to-all-start = ((bf16[8,128,8192]{2,1,0:T(8,128)(2,1)}), bf16[8,128,8192]{2,1,0:T(8,128)(2,1)}, u32[]{:S(2)}, u32[]{:S(2)}) async-start(bf16[8,128,8192]{2,1,0:T(8,128)(2,1)} %stack.2), calls=%async_computation | async-start | bytes 33554432 | tf_op jit(solution)/shard_map/all_to_all | solution.py:12
  19.1 652.0 %all-reduce.2.cloned.1.call-start = ((), (), s32[]{:S(2)}) async-start(), calls=%async_computation.1 | async-start | bytes 16777216 | tf_op jit(solution)/shard_map/psum | solution.py:46
  249.4 4.3 copy-start.1
  249.4 4.3 copy-start.2
  379.4 318.6 %copy-start = (f32[1,4,128,128]{3,2,1,0:T(8,128)S(1)}, f32[1,4,128,128]{3,2,1,0:T(8,128)}, u32[]{:S(2)}) copy-start(f32[1,4,128,128]{3,2,1,0:T(8,128)} %param.10) | copy-start | bytes 786436
Sparse Core Ops, SparseCore 0:
  379.6 291.5 all-reduce.1
